TPU v7x, 768 devices: a whole 4x8x12 slice. The times are simulated.
768 devices in a mesh: dp: 64 (over x, y, core), section: 12 (over z).
Axes of the slice: x: 4, y: 8, z: 12, core: 2. Of those that a mesh axis runs over, the one named last changes fastest.
Arguments:
- hidden_in: bfloat16 [12, 8192, 2048], P('section', 'dp'), may hold values from -80 to 80
- queries: bfloat16 [12, 8192, 2048], P('section', 'dp'), may hold values from -20 to 20
- keys: bfloat16 [12, 8192, 512], P('section', 'dp'), may hold values from -6 to 6
- segments: int32 [64, 128], P('dp'), may hold values from 0 to 3, as said below
- value_weight: bfloat16 [12, 2048, 512], P('section'), may hold values from -0.125 to 0.125
- norm_gain: float32 [12, 2048], P('section'), may hold values from 0.25 to 1.75
- upstream: bfloat16 [8192, 2048], P('dp'), may hold values from -6 to 6
Outputs:
- input_grads: bfloat16 [12, 8192, 2048], P('section', 'dp')
- value_weight_grads: float32 [12, 2048, 512], P('section', 'dp')
- gain_grads: float32 [12, 2048], P('section', 'dp')
Inputs may be any that keep to these rules, and one draw needn't show every extreme that they name: `segments`: within each aligned block of 64 list-order tokens of a replica the list ids run from 0 to 3 in order, never falling; each of the 4 lists has 1 to 48 tokens and one has exactly 48.
All inputs are finite; a program needn't handle non-finite values.
Results may differ from a plain program's by a relative error of at most 0.03.
Values may be sent and summed in bfloat16 or wider, within the bound.
A program may use at most 32 MiB of HBM per device.

v0:
```python
import jax
import jax.numpy as jnp
from jax import lax
from jax.sharding import PartitionSpec as P

KEY_VALUE_HEADS = 4
HEAD_FEATURES = 128
MICRO_ROWS = 64
MICRO = 2


epsilon = 1e-06
masked_score = -1e30


def passed_along(block, axis, distance):
    devices = range(lax.axis_size(axis))
    route = [(i - distance, i) for i in devices if i - distance in devices]
    return lax.ppermute(block, axis, route)


def attention_probs(query_tile_block, key_tile_block, list_block):
    block_row_count = query_tile_block.shape[0]
    group_width = query_tile_block.shape[1] // key_tile_block.shape[1]
    query_grid4 = query_tile_block.reshape(
        block_row_count, KEY_VALUE_HEADS, group_width, HEAD_FEATURES
    )
    key_grid3 = key_tile_block.reshape(block_row_count, KEY_VALUE_HEADS, HEAD_FEATURES)
    scores = jnp.einsum(
        "ikgd,jkd->kgij", query_grid4, key_grid3, preferred_element_type=jnp.float32
    ) * HEAD_FEATURES ** (-0.5)
    positions = lax.iota(jnp.int32, block_row_count)
    allowed = (list_block[:, None] == list_block[None, :]) & (
        positions[None, :] <= positions[:, None]
    )
    scores = jnp.where(allowed, scores, masked_score)
    exp_scores = jnp.exp(scores - jnp.max(scores, axis=-1, keepdims=True))
    return (exp_scores / jnp.sum(exp_scores, axis=-1, keepdims=True)).astype(jnp.bfloat16)


def on_device(hidden_in, queries, keys, segments, value_weight, norm_gain, upstream):
    hidden_list, query_list, key_list = (
        lax.all_to_all(hidden_in, "dp", split_axis=1, concat_axis=1, tiled=True),
        lax.all_to_all(queries, "dp", split_axis=1, concat_axis=1, tiled=True),
        lax.all_to_all(keys, "dp", split_axis=1, concat_axis=1, tiled=True),
    )
    x_rows = hidden_list[0]
    query_rows = query_list[0]
    key_rows = key_list[0]
    list_rows = segments[0]
    value_proj = value_weight[0]
    gain_row = norm_gain[0]
    row_count, model_width = x_rows.shape
    kv_width = key_rows.shape[1]
    group_width = model_width // kv_width
    section_index = lax.axis_index("section")
    section_last = lax.axis_size("section") - 1
    tick_count = MICRO + section_last
    grad_scale = float(row_count * lax.axis_size("dp")) ** (-0.5)
    x_wide = x_rows.astype(jnp.float32)
    inv_rms = lax.rsqrt(jnp.mean(x_wide * x_wide, axis=1, keepdims=True) + epsilon)
    x_norm = x_wide * inv_rms
    normed = (x_norm * gain_row).astype(jnp.bfloat16)

    def block_probs(micro_index):
        row_start = micro_index * MICRO_ROWS
        return attention_probs(
            lax.dynamic_slice_in_dim(query_rows, row_start, MICRO_ROWS, 0),
            lax.dynamic_slice_in_dim(key_rows, row_start, MICRO_ROWS, 0),
            lax.dynamic_slice_in_dim(list_rows, row_start, MICRO_ROWS, 0),
        )

    def run_block(gradient_block, micro_index, buffers):
        input_all, values_all, gain_total, weight_total = buffers
        row_start = micro_index * MICRO_ROWS
        block_weights = block_probs(micro_index)
        gradient_grid4 = gradient_block.reshape(
            MICRO_ROWS, KEY_VALUE_HEADS, group_width, HEAD_FEATURES
        )
        value_gradient = jnp.einsum(
            "kgij,ikgd->jkd", block_weights, gradient_grid4, preferred_element_type=jnp.float32
        )
        value_gradient = value_gradient.reshape(MICRO_ROWS, kv_width).astype(jnp.bfloat16)
        x_block = lax.dynamic_slice_in_dim(x_norm, row_start, MICRO_ROWS, 0)
        inv_block = lax.dynamic_slice_in_dim(inv_rms, row_start, MICRO_ROWS, 0)
        normed_grad = lax.dot_general(
            value_gradient, value_proj, (((1,), (1,)), ((), ())), preferred_element_type=jnp.float32
        )
        scaled = normed_grad * gain_row
        inner_mean = jnp.mean(x_block * scaled, axis=1, keepdims=True)
        input_grad = (
            gradient_block.astype(jnp.float32) + inv_block * (scaled - x_block * inner_mean)
        ).astype(jnp.bfloat16)
        gain_total = gain_total + jnp.sum(x_block * normed_grad, axis=0)
        normed_block = lax.dynamic_slice_in_dim(normed, row_start, MICRO_ROWS, 0)
        weight_total = weight_total + lax.dot_general(
            normed_block,
            value_gradient,
            (((0,), (0,)), ((), ())),
            preferred_element_type=jnp.float32,
        )
        input_all = lax.dynamic_update_slice_in_dim(input_all, input_grad, row_start, 0)
        values_all = lax.dynamic_update_slice_in_dim(values_all, value_gradient, row_start, 0)
        return (input_grad, (input_all, values_all, gain_total, weight_total))

    def spare_block(gradient_block, micro_index, buffers):
        return (jnp.zeros_like(gradient_block), buffers)

    def tick_step(tick_index, loop_state):
        received, buffers = loop_state
        micro_index = tick_index - (section_last - section_index)
        is_live = (micro_index >= 0) & (micro_index < MICRO)
        micro_index = jnp.clip(micro_index, 0, MICRO - 1)
        from_top = lax.dynamic_slice_in_dim(upstream, micro_index * MICRO_ROWS, MICRO_ROWS, 0)
        gradient_block = jnp.where(section_index == section_last, from_top, received)
        handed, buffers = lax.cond(
            is_live, run_block, spare_block, gradient_block, micro_index, buffers
        )
        received = passed_along(handed, "section", -1)
        return (received, buffers)

    weight_init = jnp.zeros((model_width, kv_width), jnp.float32)
    buffers = (
        jnp.zeros((row_count, model_width), jnp.bfloat16),
        jnp.zeros((row_count, kv_width), jnp.bfloat16),
        jnp.zeros((model_width,), jnp.float32),
        weight_init,
    )
    received = jnp.zeros((MICRO_ROWS, model_width), jnp.bfloat16)
    received, buffers = lax.fori_loop(0, tick_count, tick_step, (received, buffers))
    input_all, values_all, gain_total, weight_total = buffers
    input_stored = lax.all_to_all(input_all, "dp", split_axis=0, concat_axis=0, tiled=True)
    weight_sum, gain_sum = (
        lax.psum_scatter(weight_total, "dp", scatter_dimension=0, tiled=True),
        lax.psum_scatter(gain_total, "dp", scatter_dimension=0, tiled=True),
    )
    return (input_stored[None], (weight_sum * grad_scale)[None], (gain_sum * grad_scale)[None])


def solution(mesh):
    in_specs = (
        P("section", "dp", None),
        P("section", "dp", None),
        P("section", "dp", None),
        P("dp", None),
        P("section", None, None),
        P("section", None),
        P("dp", None),
    )
    out_specs = (P("section", "dp", None), P("section", "dp", None), P("section", "dp"))
    return jax.shard_map(
        on_device, mesh=mesh, in_specs=in_specs, out_specs=out_specs, check_vma=False
    )
```

profile of v0, /device:TPU:1, one launch (start us, length us, event | category | flops | bytes accessed | tf_op | source)
XLA Modules:
  0.0 596.6 jit_solution(17121168275945221826)
XLA Ops:
  8.9 1.4 reduce.1
  11.0 14.5 %all-to-all-start.1 = ((bf16[64,2,512]{2,1,0:T(2,128)(2,1)}), bf16[64,2,512]{2,1,0:T(2,128)(2,1)S(1)}, u32[]{:S(2)}, u32[]{:S(2)}) async-start(bf16[64,2,512]{2,1,0:T(2,128)(2,1)} %reshape.66), calls=%async_computation.1 | async-start | bytes 262144 | tf_op jit(solution)/shard_map/all_to_all | solution.py:45
  25.5 1.9 copy.76
  27.4 3.7 reduce
  32.2 3.8 all-to-all-done.1
  36.0 6.7 %all-to-all-start = ((bf16[64,2,2048]{2,1,0:T(2,128)(2,1)}), bf16[64,2,2048]{2,1,0:T(2,128)(2,1)S(1)}, u32[]{:S(2)}, u32[]{:S(2)}) async-start(bf16[64,2,2048]{2,1,0:T(2,128)(2,1)} %reshape.64), calls=%async_computation | async-start | bytes 1048576 | tf_op jit(solution)/shard_map/all_to_all | solution.py:43
  43.5 3.7 reduce.2
  48.4 11.6 %all-to-all-done = bf16[64,2,2048]{2,1,0:T(2,128)(2,1)S(1)} async-done(((bf16[64,2,2048]{2,1,0:T(2,128)(2,1)}), bf16[64,2,2048]{2,1,0:T(2,128)(2,1)S(1)}, u32[]{:S(2)}, u32[]{:S(2)}) %all-to-all-start) | async-done | bytes 524320 | tf_op jit(solution)/shard_map/all_to_all | solution.py:43
  60.0 6.3 %all-to-all-start.2 = ((bf16[64,2,2048]{2,1,0:T(2,128)(2,1)}), bf16[64,2,2048]{2,1,0:T(2,128)(2,1)S(1)}, u32[]{:S(2)}, u32[]{:S(2)}) async-start(bf16[64,2,2048]{2,1,0:T(2,128)(2,1)} %reshape.68), calls=%async_computation.2 | async-start | bytes 1048576 | tf_op jit(solution)/shard_map/all_to_all | solution.py:44
  68.6 15.0 %all-to-all-done.2 = bf16[64,2,2048]{2,1,0:T(2,128)(2,1)S(1)} async-done(((bf16[64,2,2048]{2,1,0:T(2,128)(2,1)}), bf16[64,2,2048]{2,1,0:T(2,128)(2,1)S(1)}, u32[]{:S(2)}, u32[]{:S(2)}) %all-to-all-start.2) | async-done | bytes 524320 | tf_op jit(solution)/shard_map/all_to_all | solution.py:44
  85.2 2.6 multiply_convert_fusion
  87.9 2.5 broadcast_in_dim.40
  91.9 340.6 %while.21 = (s32[]{:T(128)}, bf16[64,2048]{1,0:T(8,128)(2,1)}, bf16[128,2048]{1,0:T(8,128)(2,1)}, f32[2048]{0:T(1024)S(1)}, f32[2048,512]{1,0:T(8,128)}, /*index...) while((s32[]{:T(128)}, bf16[64,2048]{1,0:T(8,128)(2,1)}, ...), condition=%wide.region_8.9_spmd, body=%wide.region_1.8_spmd.sunk | while | flops 305180736 | bytes 23926400 | solution.py:130
  92.6 1.3 collective-permute-start
  93.9 8.4 %collective-permute-done = bf16[64,2048]{1,0:T(8,128)(2,1)S(1)} collective-permute-done((bf16[64,2048]{1,0:T(8,128)(2,1)}, bf16[64,2048]{1,0:T(8,128)(2,1)S(1)}, u32[]{:S(2)}, u32[]{:S(2)}) %collective-permute-start) | collective-permute-done | bytes 262176 | tf_op jit(solution)/shard_map/while/body/eval_jaxpr/ppermute | solution.py:19
  103.7 1.3 collective-permute-start
  105.0 7.5 %collective-permute-done = bf16[64,2048]{1,0:T(8,128)(2,1)S(1)} collective-permute-done((bf16[64,2048]{1,0:T(8,128)(2,1)}, bf16[64,2048]{1,0:T(8,128)(2,1)S(1)}, u32[]{:S(2)}, u32[]{:S(2)}) %collective-permute-start) | collective-permute-done | bytes 262176 | tf_op jit(solution)/shard_map/while/body/eval_jaxpr/ppermute | solution.py:19
  113.9 1.3 collective-permute-start
  115.2 6.5 %collective-permute-done = bf16[64,2048]{1,0:T(8,128)(2,1)S(1)} collective-permute-done((bf16[64,2048]{1,0:T(8,128)(2,1)}, bf16[64,2048]{1,0:T(8,128)(2,1)S(1)}, u32[]{:S(2)}, u32[]{:S(2)}) %collective-permute-start) | collective-permute-done | bytes 262176 | tf_op jit(solution)/shard_map/while/body/eval_jaxpr/ppermute | solution.py:19
  123.2 1.3 collective-permute-start
  124.5 9.5 %collective-permute-done = bf16[64,2048]{1,0:T(8,128)(2,1)S(1)} collective-permute-done((bf16[64,2048]{1,0:T(8,128)(2,1)}, bf16[64,2048]{1,0:T(8,128)(2,1)S(1)}, u32[]{:S(2)}, u32[]{:S(2)}) %collective-permute-start) | collective-permute-done | bytes 262176 | tf_op jit(solution)/shard_map/while/body/eval_jaxpr/ppermute | solution.py:19
  135.4 1.3 collective-permute-start
  136.7 6.3 %collective-permute-done = bf16[64,2048]{1,0:T(8,128)(2,1)S(1)} collective-permute-done((bf16[64,2048]{1,0:T(8,128)(2,1)}, bf16[64,2048]{1,0:T(8,128)(2,1)S(1)}, u32[]{:S(2)}, u32[]{:S(2)}) %collective-permute-start) | collective-permute-done | bytes 262176 | tf_op jit(solution)/shard_map/while/body/eval_jaxpr/ppermute | solution.py:19
  144.4 1.3 collective-permute-start
  145.7 6.5 %collective-permute-done = bf16[64,2048]{1,0:T(8,128)(2,1)S(1)} collective-permute-done((bf16[64,2048]{1,0:T(8,128)(2,1)}, bf16[64,2048]{1,0:T(8,128)(2,1)S(1)}, u32[]{:S(2)}, u32[]{:S(2)}) %collective-permute-start) | collective-permute-done | bytes 262176 | tf_op jit(solution)/shard_map/while/body/eval_jaxpr/ppermute | solution.py:19
  153.6 1.3 collective-permute-start
  154.9 7.2 %collective-permute-done = bf16[64,2048]{1,0:T(8,128)(2,1)S(1)} collective-permute-done((bf16[64,2048]{1,0:T(8,128)(2,1)}, bf16[64,2048]{1,0:T(8,128)(2,1)S(1)}, u32[]{:S(2)}, u32[]{:S(2)}) %collective-permute-start) | collective-permute-done | bytes 262176 | tf_op jit(solution)/shard_map/while/body/eval_jaxpr/ppermute | solution.py:19
  164.9 7.2 %collective-permute-done = bf16[64,2048]{1,0:T(8,128)(2,1)S(1)} collective-permute-done((bf16[64,2048]{1,0:T(8,128)(2,1)}, bf16[64,2048]{1,0:T(8,128)(2,1)S(1)}, u32[]{:S(2)}, u32[]{:S(2)}) %collective-permute-start) | collective-permute-done | bytes 262176 | tf_op jit(solution)/shard_map/while/body/eval_jaxpr/ppermute | solution.py:19
  174.9 7.2 %collective-permute-done = bf16[64,2048]{1,0:T(8,128)(2,1)S(1)} collective-permute-done((bf16[64,2048]{1,0:T(8,128)(2,1)}, bf16[64,2048]{1,0:T(8,128)(2,1)S(1)}, u32[]{:S(2)}, u32[]{:S(2)}) %collective-permute-start) | collective-permute-done | bytes 262176 | tf_op jit(solution)/shard_map/while/body/eval_jaxpr/ppermute | solution.py:19
  184.8 8.1 %collective-permute-done = bf16[64,2048]{1,0:T(8,128)(2,1)S(1)} collective-permute-done((bf16[64,2048]{1,0:T(8,128)(2,1)}, bf16[64,2048]{1,0:T(8,128)(2,1)S(1)}, u32[]{:S(2)}, u32[]{:S(2)}) %collective-permute-start) | collective-permute-done | bytes 262176 | tf_op jit(solution)/shard_map/while/body/eval_jaxpr/ppermute | solution.py:19
  195.7 183.9 %collective-permute-done = bf16[64,2048]{1,0:T(8,128)(2,1)S(1)} collective-permute-done((bf16[64,2048]{1,0:T(8,128)(2,1)}, bf16[64,2048]{1,0:T(8,128)(2,1)S(1)}, u32[]{:S(2)}, u32[]{:S(2)}) %collective-permute-start) | collective-permute-done | bytes 262176 | tf_op jit(solution)/shard_map/while/body/eval_jaxpr/ppermute | solution.py:19
  380.3 17.5 %conditional.2 = (bf16[64,2048]{1,0:T(8,128)(2,1)}, bf16[128,2048]{1,0:T(8,128)(2,1)}, f32[2048]{0:T(1024)S(1)}, f32[2048,512]{1,0:T(8,128)}) conditional(s32[]{:T(128)} %convert_element_type.59, (bf16[128,2048]{1,0:T(8,128)(2,1)}, f32[2048]{0:T(1024)S(1)}, f32[2048,512]{1,0:T(8,128)}) %tuple.64, (pred[]{:T(512)}, s32[]{:T(128)}, ...), branch_computations={%region_2.2_spmd, %region_3.7_spmd} | conditional | flops 305180736 | bytes 21828824 | solution.py:116
  380.3 1.9 dynamic-slice_select_fusion
  382.2 1.8 reshape.58
  385.7 2.2 fusion.33
  388.8 1.3 fusion.6
  390.1 5.0 convolution_add_fusion
  399.1 7.2 %collective-permute-done = bf16[64,2048]{1,0:T(8,128)(2,1)S(1)} collective-permute-done((bf16[64,2048]{1,0:T(8,128)(2,1)}, bf16[64,2048]{1,0:T(8,128)(2,1)S(1)}, u32[]{:S(2)}, u32[]{:S(2)}) %collective-permute-start) | collective-permute-done | bytes 262176 | tf_op jit(solution)/shard_map/while/body/eval_jaxpr/ppermute | solution.py:19
  407.0 17.5 %conditional.2 = (bf16[64,2048]{1,0:T(8,128)(2,1)}, bf16[128,2048]{1,0:T(8,128)(2,1)}, f32[2048]{0:T(1024)S(1)}, f32[2048,512]{1,0:T(8,128)}) conditional(s32[]{:T(128)} %convert_element_type.59, (bf16[128,2048]{1,0:T(8,128)(2,1)}, f32[2048]{0:T(1024)S(1)}, f32[2048,512]{1,0:T(8,128)}) %tuple.64, (pred[]{:T(512)}, s32[]{:T(128)}, ...), branch_computations={%region_2.2_spmd, %region_3.7_spmd} | conditional | flops 305180736 | bytes 21828824 | solution.py:116
  407.0 1.9 dynamic-slice_select_fusion
  408.9 1.8 reshape.58
  412.4 2.2 fusion.33
  415.5 1.3 fusion.6
  416.9 5.0 convolution_add_fusion
  425.8 6.0 %collective-permute-done = bf16[64,2048]{1,0:T(8,128)(2,1)S(1)} collective-permute-done((bf16[64,2048]{1,0:T(8,128)(2,1)}, bf16[64,2048]{1,0:T(8,128)(2,1)S(1)}, u32[]{:S(2)}, u32[]{:S(2)}) %collective-permute-start) | collective-permute-done | bytes 262176 | tf_op jit(solution)/shard_map/while/body/eval_jaxpr/ppermute | solution.py:19
  434.7 17.8 %all-to-all-start.3 = ((bf16[64,2,2048]{2,1,0:T(2,128)(2,1)}), bf16[64,2,2048]{2,1,0:T(2,128)(2,1)S(1)}, u32[]{:S(2)}, u32[]{:S(2)}) async-start(bf16[64,2,2048]{2,1,0:T(2,128)(2,1)} %all_to_all.18), calls=%async_computation.3 | async-start | bytes 1048576 | tf_op jit(solution)/shard_map/all_to_all | solution.py:132
  454.4 131.6 %all-reduce = f32[2048]{0:T(1024)S(1)} all-reduce(f32[2048]{0:T(1024)S(1)} %get-tuple-element.511), channel_id=3, replica_groups=mesh['dp'=64,'section'=12] {'dp'}, use_global_device_ids=true, to_apply=%region_10.11.clone | all-reduce | flops 2048 | bytes 16384
  588.2 1.5 multiply_bitcast_fusion
  (120 shorter events, 60.0 us)
Async XLA Ops:
  7.2 35.5 %copy-start.7 = (bf16[1,128,2048]{2,1,0:T(8,128)(2,1)S(1)}, bf16[1,128,2048]{2,1,0:T(8,128)(2,1)}, u32[]{:S(2)}) copy-start(bf16[1,128,2048]{2,1,0:T(8,128)(2,1)} %param.12) | copy-start | bytes 1572868
  11.0 25.0 %all-to-all-start.1 = ((bf16[64,2,512]{2,1,0:T(2,128)(2,1)}), bf16[64,2,512]{2,1,0:T(2,128)(2,1)S(1)}, u32[]{:S(2)}, u32[]{:S(2)}) async-start(bf16[64,2,512]{2,1,0:T(2,128)(2,1)} %reshape.66), calls=%async_computation.1 | async-start | bytes 262144 | tf_op jit(solution)/shard_map/all_to_all | solution.py:45
  36.0 24.0 %all-to-all-start = ((bf16[64,2,2048]{2,1,0:T(2,128)(2,1)}), bf16[64,2,2048]{2,1,0:T(2,128)(2,1)S(1)}, u32[]{:S(2)}, u32[]{:S(2)}) async-start(bf16[64,2,2048]{2,1,0:T(2,128)(2,1)} %reshape.64), calls=%async_computation | async-start | bytes 1048576 | tf_op jit(solution)/shard_map/all_to_all | solution.py:43
  47.2 38.0 %copy-start.6 = (f32[1,2048]{1,0:T(1,128)S(1)}, f32[1,2048]{1,0:T(1,128)}, u32[]{:S(2)}) copy-start(f32[1,2048]{1,0:T(1,128)} %param.16) | copy-start | bytes 24580
  60.0 23.6 %all-to-all-start.2 = ((bf16[64,2,2048]{2,1,0:T(2,128)(2,1)}), bf16[64,2,2048]{2,1,0:T(2,128)(2,1)S(1)}, u32[]{:S(2)}, u32[]{:S(2)}) async-start(bf16[64,2,2048]{2,1,0:T(2,128)(2,1)} %reshape.68), calls=%async_computation.2 | async-start | bytes 1048576 | tf_op jit(solution)/shard_map/all_to_all | solution.py:44
  66.3 522.0 %reduce-scatter.2.cloned.1.call-start = ((), (), s32[]{:S(2)}) async-start(), calls=%async_computation.5 | async-start | bytes 4259840 | tf_op jit(solution)/shard_map/reduce_scatter | solution.py:134
  67.6 16.5 %copy-start.1 = (bf16[128,1,2048]{2,1,0:T(2,128)(2,1)}, bf16[128,1,2048]{2,1,0:T(2,128)(2,1)S(1)}, u32[]{:S(2)}) copy-start(bf16[128,1,2048]{2,1,0:T(2,128)(2,1)S(1)} %reshape.65) | copy-start | bytes 1572868
  85.2 6.7 %copy-start = (bf16[1,2048,512]{2,1,0:T(8,128)(2,1)S(1)}, bf16[1,2048,512]{2,1,0:T(8,128)(2,1)}, u32[]{:S(2)}) copy-start(bf16[1,2048,512]{2,1,0:T(8,128)(2,1)} %param.15) | copy-start | bytes 6291460
  92.6 9.7 %collective-permute-start = (bf16[64,2048]{1,0:T(8,128)(2,1)}, bf16[64,2048]{1,0:T(8,128)(2,1)S(1)}, u32[]{:S(2)}, u32[]{:S(2)}) collective-permute-start(bf16[64,2048]{1,0:T(8,128)(2,1)} %get-tuple-element.658), channel_id=1, source_target_pairs={{1,0},{2,1},{3,2},{4,3},{5,4},{6,5},{7,6},{8,7},{9,8},{10,9},{11,1... | collective-permute-start | bytes 786440 | tf_op jit(solution)/shard_map/while/body/eval_jaxpr/ppermute | solution.py:19
  102.3 0.7 copy-start.2
  103.7 8.7 %collective-permute-start = (bf16[64,2048]{1,0:T(8,128)(2,1)}, bf16[64,2048]{1,0:T(8,128)(2,1)S(1)}, u32[]{:S(2)}, u32[]{:S(2)}) collective-permute-start(bf16[64,2048]{1,0:T(8,128)(2,1)} %get-tuple-element.658), channel_id=1, source_target_pairs={{1,0},{2,1},{3,2},{4,3},{5,4},{6,5},{7,6},{8,7},{9,8},{10,9},{11,1... | collective-permute-start | bytes 786440 | tf_op jit(solution)/shard_map/while/body/eval_jaxpr/ppermute | solution.py:19
  112.5 0.7 copy-start.2
  113.9 7.8 %collective-permute-start = (bf16[64,2048]{1,0:T(8,128)(2,1)}, bf16[64,2048]{1,0:T(8,128)(2,1)S(1)}, u32[]{:S(2)}, u32[]{:S(2)}) collective-permute-start(bf16[64,2048]{1,0:T(8,128)(2,1)} %get-tuple-element.658), channel_id=1, source_target_pairs={{1,0},{2,1},{3,2},{4,3},{5,4},{6,5},{7,6},{8,7},{9,8},{10,9},{11,1... | collective-permute-start | bytes 786440 | tf_op jit(solution)/shard_map/while/body/eval_jaxpr/ppermute | solution.py:19
  121.8 0.7 copy-start.2
  123.2 10.8 %collective-permute-start = (bf16[64,2048]{1,0:T(8,128)(2,1)}, bf16[64,2048]{1,0:T(8,128)(2,1)S(1)}, u32[]{:S(2)}, u32[]{:S(2)}) collective-permute-start(bf16[64,2048]{1,0:T(8,128)(2,1)} %get-tuple-element.658), channel_id=1, source_target_pairs={{1,0},{2,1},{3,2},{4,3},{5,4},{6,5},{7,6},{8,7},{9,8},{10,9},{11,1... | collective-permute-start | bytes 786440 | tf_op jit(solution)/shard_map/while/body/eval_jaxpr/ppermute | solution.py:19
  134.0 0.7 copy-start.2
  135.4 7.6 %collective-permute-start = (bf16[64,2048]{1,0:T(8,128)(2,1)}, bf16[64,2048]{1,0:T(8,128)(2,1)S(1)}, u32[]{:S(2)}, u32[]{:S(2)}) collective-permute-start(bf16[64,2048]{1,0:T(8,128)(2,1)} %get-tuple-element.658), channel_id=1, source_target_pairs={{1,0},{2,1},{3,2},{4,3},{5,4},{6,5},{7,6},{8,7},{9,8},{10,9},{11,1... | collective-permute-start | bytes 786440 | tf_op jit(solution)/shard_map/while/body/eval_jaxpr/ppermute | solution.py:19
  143.0 0.7 copy-start.2
  144.4 7.8 %collective-permute-start = (bf16[64,2048]{1,0:T(8,128)(2,1)}, bf16[64,2048]{1,0:T(8,128)(2,1)S(1)}, u32[]{:S(2)}, u32[]{:S(2)}) collective-permute-start(bf16[64,2048]{1,0:T(8,128)(2,1)} %get-tuple-element.658), channel_id=1, source_target_pairs={{1,0},{2,1},{3,2},{4,3},{5,4},{6,5},{7,6},{8,7},{9,8},{10,9},{11,1... | collective-permute-start | bytes 786440 | tf_op jit(solution)/shard_map/while/body/eval_jaxpr/ppermute | solution.py:19
  152.2 0.7 copy-start.2
  153.6 8.5 %collective-permute-start = (bf16[64,2048]{1,0:T(8,128)(2,1)}, bf16[64,2048]{1,0:T(8,128)(2,1)S(1)}, u32[]{:S(2)}, u32[]{:S(2)}) collective-permute-start(bf16[64,2048]{1,0:T(8,128)(2,1)} %get-tuple-element.658), channel_id=1, source_target_pairs={{1,0},{2,1},{3,2},{4,3},{5,4},{6,5},{7,6},{8,7},{9,8},{10,9},{11,1... | collective-permute-start | bytes 786440 | tf_op jit(solution)/shard_map/while/body/eval_jaxpr/ppermute | solution.py:19
  162.2 0.7 copy-start.2
  163.6 8.5 %collective-permute-start = (bf16[64,2048]{1,0:T(8,128)(2,1)}, bf16[64,2048]{1,0:T(8,128)(2,1)S(1)}, u32[]{:S(2)}, u32[]{:S(2)}) collective-permute-start(bf16[64,2048]{1,0:T(8,128)(2,1)} %get-tuple-element.658), channel_id=1, source_target_pairs={{1,0},{2,1},{3,2},{4,3},{5,4},{6,5},{7,6},{8,7},{9,8},{10,9},{11,1... | collective-permute-start | bytes 786440 | tf_op jit(solution)/shard_map/while/body/eval_jaxpr/ppermute | solution.py:19
  172.1 0.7 copy-start.2
  173.6 8.5 %collective-permute-start = (bf16[64,2048]{1,0:T(8,128)(2,1)}, bf16[64,2048]{1,0:T(8,128)(2,1)S(1)}, u32[]{:S(2)}, u32[]{:S(2)}) collective-permute-start(bf16[64,2048]{1,0:T(8,128)(2,1)} %get-tuple-element.658), channel_id=1, source_target_pairs={{1,0},{2,1},{3,2},{4,3},{5,4},{6,5},{7,6},{8,7},{9,8},{10,9},{11,1... | collective-permute-start | bytes 786440 | tf_op jit(solution)/shard_map/while/body/eval_jaxpr/ppermute | solution.py:19
  182.1 0.7 copy-start.2
  183.5 9.4 %collective-permute-start = (bf16[64,2048]{1,0:T(8,128)(2,1)}, bf16[64,2048]{1,0:T(8,128)(2,1)S(1)}, u32[]{:S(2)}, u32[]{:S(2)}) collective-permute-start(bf16[64,2048]{1,0:T(8,128)(2,1)} %get-tuple-element.658), channel_id=1, source_target_pairs={{1,0},{2,1},{3,2},{4,3},{5,4},{6,5},{7,6},{8,7},{9,8},{10,9},{11,1... | collective-permute-start | bytes 786440 | tf_op jit(solution)/shard_map/while/body/eval_jaxpr/ppermute | solution.py:19
  192.9 0.7 copy-start.2
  194.4 185.2 %collective-permute-start = (bf16[64,2048]{1,0:T(8,128)(2,1)}, bf16[64,2048]{1,0:T(8,128)(2,1)S(1)}, u32[]{:S(2)}, u32[]{:S(2)}) collective-permute-start(bf16[64,2048]{1,0:T(8,128)(2,1)} %get-tuple-element.658), channel_id=1, source_target_pairs={{1,0},{2,1},{3,2},{4,3},{5,4},{6,5},{7,6},{8,7},{9,8},{10,9},{11,1... | collective-permute-start | bytes 786440 | tf_op jit(solution)/shard_map/while/body/eval_jaxpr/ppermute | solution.py:19
  379.6 0.7 copy-start.2
  390.1 5.9 copy-start.8
  390.1 6.0 %copy-start.3 = (bf16[128,2048]{1,0:T(8,128)(2,1)S(1)}, bf16[128,2048]{1,0:T(8,128)(2,1)}, u32[]{:S(2)}) copy-start(bf16[128,2048]{1,0:T(8,128)(2,1)} %get-tuple-element.478) | copy-start | bytes 1572868 | tf_op jit(solution)/shard_map/while/body/eval_jaxpr/cond
  397.0 0.8 copy-start.4
  397.8 8.5 %collective-permute-start = (bf16[64,2048]{1,0:T(8,128)(2,1)}, bf16[64,2048]{1,0:T(8,128)(2,1)S(1)}, u32[]{:S(2)}, u32[]{:S(2)}) collective-permute-start(bf16[64,2048]{1,0:T(8,128)(2,1)} %get-tuple-element.658), channel_id=1, source_target_pairs={{1,0},{2,1},{3,2},{4,3},{5,4},{6,5},{7,6},{8,7},{9,8},{10,9},{11,1... | collective-permute-start | bytes 786440 | tf_op jit(solution)/shard_map/while/body/eval_jaxpr/ppermute | solution.py:19
  406.3 0.7 copy-start.2
  416.9 5.9 copy-start.8
  416.9 6.0 %copy-start.3 = (bf16[128,2048]{1,0:T(8,128)(2,1)S(1)}, bf16[128,2048]{1,0:T(8,128)(2,1)}, u32[]{:S(2)}) copy-start(bf16[128,2048]{1,0:T(8,128)(2,1)} %get-tuple-element.478) | copy-start | bytes 1572868 | tf_op jit(solution)/shard_map/while/body/eval_jaxpr/cond
  423.7 0.8 copy-start.4
  424.5 7.3 %collective-permute-start = (bf16[64,2048]{1,0:T(8,128)(2,1)}, bf16[64,2048]{1,0:T(8,128)(2,1)S(1)}, u32[]{:S(2)}, u32[]{:S(2)}) collective-permute-start(bf16[64,2048]{1,0:T(8,128)(2,1)} %get-tuple-element.658), channel_id=1, source_target_pairs={{1,0},{2,1},{3,2},{4,3},{5,4},{6,5},{7,6},{8,7},{9,8},{10,9},{11,1... | collective-permute-start | bytes 786440 | tf_op jit(solution)/shard_map/while/body/eval_jaxpr/ppermute | solution.py:19
  431.8 0.7 copy-start.2
  432.6 1.0 copy-start.5
  434.7 151.9 %all-to-all-start.3 = ((bf16[64,2,2048]{2,1,0:T(2,128)(2,1)}), bf16[64,2,2048]{2,1,0:T(2,128)(2,1)S(1)}, u32[]{:S(2)}, u32[]{:S(2)}) async-start(bf16[64,2,2048]{2,1,0:T(2,128)(2,1)} %all_to_all.18), calls=%async_computation.3 | async-start | bytes 1048576 | tf_op jit(solution)/shard_map/all_to_all | solution.py:132
Sparse Core Ops, SparseCore 0:
  432.7 155.4 reduce-scatter.1
where the time goes:
time: 602 us; the launch traced here: 597 us
  waiting for transfers between devices  303 us (50%)
  blocking collectives  132 us (22%)
  starting transfers between devices  61.9 us (10%)
  local copies, waits for them, and re-layouts  46.4 us (8%)
  other arithmetic  20.2 us (3%)
  matrix products  18.8 us (3%)
  between operations  14.8 us (2%)
    ppermute x13, waiting for transfers between devices, passed_along(): return lax.ppermute(block, axis, route)  272 us
    unnamed x1, blocking collectives  132 us
    all_to_all x1, starting transfers between devices, on_device(): lax.all_to_all(input_all, 'dp', split_axis=0, concat_axis=0, tiled=True)  17.8 us
    ppermute x13, starting transfers between devices, passed_along(): return lax.ppermute(block, axis, route)  16.6 us
    all_to_all x1, waiting for transfers between devices, on_device(): lax.all_to_all(queries, 'dp', split_axis=1, concat_axis=1, tiled=True)  15 us
    all_to_all x1, starting transfers between devices, on_device(): lax.all_to_all(keys, 'dp', split_axis=1, concat_axis=1, tiled=True)  14.5 us
    unnamed x23, local copies, waits for them, and re-layouts  12.5 us
  transfers between devices with their start and end apart: 18, of which 17 were waited for; matrix products, arithmetic and copies ran while one was open for 3% of the time, Pallas kernels for 0%

commit v1 on v0

v1 whole, which is shorter than its diff:
```python
import functools

import jax
import jax.numpy as jnp
from jax import lax
from jax.experimental import pallas as pl
from jax.experimental.pallas import tpu as pltpu
from jax.sharding import PartitionSpec as P

HEADS = 16
KV = 4
GROUP = HEADS // KV
HF = 128
D = HEADS * HF
KW = KV * HF
ROWS = 64
MICRO = 2
TOK = ROWS * MICRO
PR = 16
PIECES = TOK // PR
PER = ROWS // PR
EPS = 1e-06
MASKED = -1e30
XS = 4
MESH = pl.DeviceIdType.MESH
F32 = jnp.float32
BF = jnp.bfloat16


def dot(a, b, dims=(((1,), (0,)), ((), ()))):
    return lax.dot_general(a, b, dims, preferred_element_type=F32)


NT = (((1,), (1,)), ((), ()))


def rows_of(i, n):
    return pl.ds(pl.multiple_of(i * n, n), n)


def kernel(
    nx, ny, nz,
    x_ref, q_ref, k_ref, segc_ref, segr_ref, w_ref, gain_ref, up_ref,
    out_ref, csum_ref,
    gin, gs, pt, yv, inv, wt, xs, xst, us, cst, part,
    up_sem, gin_sem, gout_sem, xs_recv, xs_send, us_recv, us_send, part_recv, part_send,
):
    me = lax.axis_index("dp")
    sec = lax.axis_index("section")
    core = lax.rem(me, 2)
    my_y = lax.rem(lax.div(me, 2), ny)
    my_x = lax.div(me, 2 * ny)
    last = nz - 1
    slots = 2 * nx
    fw = D // slots
    fo = D // (2 * nx * ny)
    slot = my_x * 2 + core

    def dev(x, y, c):
        return (x * ny + y) * 2 + c

    barrier = pltpu.get_barrier_semaphore()
    total = 0
    for dx in range(nx):
        for dy in range(ny):
            for dc in range(2):
                if (dx == 0 or dy == 0) and dx + dy + dc > 0:
                    target = dev(
                        lax.rem(my_x + dx, nx), lax.rem(my_y + dy, ny), lax.rem(core + dc, 2)
                    )
                    pl.semaphore_signal(
                        barrier, inc=1, device_id=(target, sec), device_id_type=MESH
                    )
                    total += 1

    @pl.when(sec > 0)
    def _():
        pl.semaphore_signal(barrier, inc=1, device_id=(me, sec - 1), device_id_type=MESH)

    @pl.when(sec < last)
    def _():
        pl.semaphore_signal(barrier, inc=1, device_id=(me, sec + 1), device_id_type=MESH)

    up_copy = pltpu.make_async_copy(up_ref, gin, up_sem)

    @pl.when(sec == last)
    def _():
        up_copy.start()

    gain = gain_ref[...]

    @pl.loop(0, PIECES)
    def _(i):
        xf = x_ref[rows_of(i, PR), :].astype(F32)
        r = lax.rsqrt(jnp.sum(xf * xf, axis=1, keepdims=True) * (1.0 / D) + EPS)
        inv[rows_of(i, PR), :] = r

    xg = (x_ref[...].astype(F32) * gain).astype(BF)
    yv[...] = dot(xg, w_ref[...]) * (1.0 / D)
    gs[...] = jnp.zeros_like(gs)

    def probs(m, _):
        segc = segc_ref[rows_of(m, ROWS), :]
        segr = segr_ref[m]
        j = lax.broadcasted_iota(jnp.int32, (ROWS, GROUP * ROWS), 0)
        i = lax.rem(lax.broadcasted_iota(jnp.int32, (ROWS, GROUP * ROWS), 1), ROWS)
        allowed = (segc == segr) & (j <= i)
        for c in range(KV):
            kc = k_ref[rows_of(m, ROWS), c * HF:(c + 1) * HF]
            qc = jnp.concatenate(
                [
                    q_ref[rows_of(m, ROWS), (c * GROUP + h) * HF:(c * GROUP + h + 1) * HF]
                    for h in range(GROUP)
                ],
                axis=0,
            )
            s = dot(kc, qc, NT) * HF ** (-0.5)
            s = jnp.where(allowed, s, MASKED)
            e = jnp.exp(s - jnp.max(s, axis=0, keepdims=True))
            pt[m, c] = (e / jnp.sum(e, axis=0, keepdims=True)).astype(BF)
        return 0

    lax.fori_loop(0, MICRO, probs, 0)

    for i in range(D // HF):
        wt[:, i * HF:(i + 1) * HF] = w_ref[i * HF:(i + 1) * HF, :].T

    neighbours = (sec > 0).astype(jnp.int32) + (sec < last).astype(jnp.int32)
    pl.semaphore_wait(barrier, total + neighbours)

    def peer(step):
        p = lax.rem(slot + step, slots)
        px = lax.div(p, 2)
        pc = lax.rem(p, 2)
        return p, dev(px, my_y, pc)

    def x_copy(step):
        p, target = peer(step)
        return pltpu.make_async_remote_copy(
            src_ref=x_ref.at[:, pl.ds(pl.multiple_of(p * fw, fw), fw)],
            dst_ref=xs.at[slot],
            send_sem=xs_send.at[step],
            recv_sem=xs_recv,
            device_id=(target, sec),
            device_id_type=MESH,
        )

    for step in range(1, slots):
        x_copy(step).start()
    own_x = pltpu.make_async_copy(
        x_ref.at[:, pl.ds(pl.multiple_of(slot * fw, fw), fw)], xs.at[slot], xs_recv
    )
    own_x.start()

    def turn_x():
        pltpu.make_async_copy(xs, xs, xs_recv).wait()
        for i in range(slots):
            xst[:, i * TOK:(i + 1) * TOK] = xs[i].T

    @pl.when(sec < last)
    def _():
        turn_x()

    @pl.when(sec == last)
    def _():
        up_copy.wait()

    def g_copy(ci):
        return pltpu.make_async_remote_copy(
            src_ref=out_ref.at[ci],
            dst_ref=gin.at[ci],
            send_sem=gout_sem.at[ci],
            recv_sem=gin_sem.at[ci],
            device_id=(me, lax.max(sec - 1, 0)),
            device_id_type=MESH,
        )

    def u_copy(ci, step):
        p, target = peer(step)
        return pltpu.make_async_remote_copy(
            src_ref=us.at[slot, rows_of(ci, PR), :],
            dst_ref=us.at[slot, rows_of(ci, PR), :],
            send_sem=us_send.at[ci, step],
            recv_sem=us_recv,
            device_id=(target, sec),
            device_id_type=MESH,
        )

    def chain(t, _):
        m = lax.rem(t, MICRO)
        b = PER - 1 - lax.div(t, MICRO)
        ci = m * PER + b

        @pl.when(sec < last)
        def _():
            pltpu.make_async_copy(out_ref.at[ci], gin.at[ci], gin_sem.at[ci]).wait()

        g = gin[ci]
        for h in range(HEADS):
            c, hh = divmod(h, GROUP)
            gs[m, c, pl.ds(pl.multiple_of(hh * ROWS + b * PR, PR), PR), :] = g[:, h * HF:(h + 1) * HF]
        v = jnp.concatenate(
            [dot(pt[m, c, rows_of(b, PR), :], gs[m, c]) for c in range(KV)], axis=1
        ).astype(BF)
        r = inv[rows_of(ci, PR), :]
        uf = v.astype(F32) * r
        u = uf.astype(BF)
        coef = jnp.sum(uf * yv[rows_of(ci, PR), :], axis=1, keepdims=True) * (r * r)
        ng = dot(u, wt[...])
        xf = x_ref[rows_of(ci, PR), :].astype(F32)
        out_ref[ci] = (g.astype(F32) + (gain * ng - xf * coef)).astype(BF)

        @pl.when(sec > 0)
        def _():
            g_copy(ci).start()

        us[slot, rows_of(ci, PR), :] = u
        for step in range(1, slots):
            u_copy(ci, step).start()
        return 0

    lax.fori_loop(0, PIECES, chain, 0)

    @pl.when(sec == last)
    def _():
        turn_x()

    others = us.at[pl.ds(0, slots - 1)]
    pltpu.make_async_copy(others, others, us_recv).wait()
    acc = dot(xst[...], us[...].reshape(slots * TOK, KW))
    cst[...] = acc.astype(BF).reshape(ny, fo, KW)

    def part_copy(j):
        yl, c = divmod(j, 2)
        target = dev(my_x, core * (ny // 2) + yl, c)
        return target, pltpu.make_async_remote_copy(
            src_ref=cst.at[j],
            dst_ref=part.at[my_y],
            send_sem=part_send.at[j],
            recv_sem=part_recv,
            device_id=(target, sec),
            device_id_type=MESH,
        )

    for j in range(ny):
        target, copy = part_copy(j)

        @pl.when(target != me)
        def _():
            copy.start()

        @pl.when(target == me)
        def _():
            pltpu.make_async_copy(cst.at[j], part.at[my_y], part_recv).start()

    pltpu.make_async_copy(part, part, part_recv).wait()
    total_c = part[0].astype(F32)
    for y in range(1, ny):
        total_c = total_c + part[y].astype(F32)
    csum_ref[...] = total_c

    for step in range(1, slots):
        x_copy(step).wait_send()
    def drain(ci, _):
        for step in range(1, slots):
            u_copy(ci, step).wait_send()

        @pl.when(sec > 0)
        def _():
            g_copy(ci).wait_send()

        return 0

    lax.fori_loop(0, PIECES, drain, 0)
    for j in range(ny):
        target, copy = part_copy(j)

        @pl.when(target != me)
        def _():
            copy.wait_send()


def backward(nx, ny, nz, x, q, k, segc, segr, w, gain, up):
    slots = 2 * nx
    fw = D // slots
    fo = D // (2 * nx * ny)
    vmem = pl.BlockSpec(memory_space=pltpu.VMEM)
    sem = pltpu.SemaphoreType.DMA
    return pl.pallas_call(
        functools.partial(kernel, nx, ny, nz),
        out_shape=(
            jax.ShapeDtypeStruct((PIECES, PR, D), BF),
            jax.ShapeDtypeStruct((fo, KW), F32),
        ),
        in_specs=[vmem] * 7 + [pl.BlockSpec(memory_space=pl.ANY)],
        out_specs=(vmem, vmem),
        scratch_shapes=[
            pltpu.VMEM((PIECES, PR, D), BF),
            pltpu.VMEM((MICRO, KV, GROUP * ROWS, HF), BF),
            pltpu.VMEM((MICRO, KV, ROWS, GROUP * ROWS), BF),
            pltpu.VMEM((TOK, KW), F32),
            pltpu.VMEM((TOK, 1), F32),
            pltpu.VMEM((KW, D), BF),
            pltpu.VMEM((slots, TOK, fw), BF),
            pltpu.VMEM((fw, slots * TOK), BF),
            pltpu.VMEM((slots, TOK, KW), BF),
            pltpu.VMEM((ny, fo, KW), BF),
            pltpu.VMEM((ny, fo, KW), BF),
            sem,
            sem((PIECES,)),
            sem((PIECES,)),
            sem,
            sem((slots,)),
            sem,
            sem((PIECES, slots)),
            sem,
            sem((ny,)),
        ],
        compiler_params=pltpu.CompilerParams(collective_id=0, has_side_effects=True, vmem_limit_bytes=60000 * 1024),
        name="chain",
    )(x, q, k, segc, segr, w, gain, up)


def on_device(nx, ny, nz, hidden_in, queries, keys, segments, value_weight, norm_gain, upstream):
    regroup = functools.partial(
        lax.all_to_all, axis_name="dp", split_axis=1, concat_axis=1, tiled=True
    )
    k = regroup(keys)[0]
    q = regroup(queries)[0]
    x = regroup(hidden_in)[0]
    segc = segments.reshape(TOK, 1)
    segr = jnp.tile(segments.reshape(MICRO, 1, ROWS), (1, 1, GROUP))
    w = value_weight[0]
    out, csum = backward(
        nx, ny, nz, x, q, k, segc, segr, w, norm_gain, upstream.reshape(PIECES, PR, D)
    )
    stored = lax.all_to_all(out.reshape(TOK, D), "dp", split_axis=0, concat_axis=0, tiled=True)
    fo = csum.shape[0]
    scale = float(TOK * 2 * nx * ny) ** (-0.5)
    start = lax.axis_index("dp") * fo
    own_gain = lax.dynamic_slice_in_dim(norm_gain[0], start, fo, 0)
    own_w = lax.dynamic_slice_in_dim(w, start, fo, 0).astype(F32)
    weight = csum * (own_gain[:, None] * scale)
    gains = jnp.sum(csum * own_w, axis=1) * scale
    return stored[None], weight[None], gains[None]


def solution(mesh):
    ndp = mesh.shape["dp"]
    nx = XS
    ny = ndp // (2 * nx)
    in_specs = (
        P("section", "dp", None),
        P("section", "dp", None),
        P("section", "dp", None),
        P("dp", None),
        P("section", None, None),
        P("section", None),
        P("dp", None),
    )
    out_specs = (P("section", "dp", None), P("section", "dp", None), P("section", "dp"))
    return jax.shard_map(
        functools.partial(on_device, nx, ny, mesh.shape["section"]),
        mesh=mesh, in_specs=in_specs, out_specs=out_specs, check_vma=False,
    )
```

time: 602 us -> 194 us (0.32)
  waiting for transfers between devices: 303 us -> 43.1 us
  blocking collectives: 132 us -> 0 us
  Pallas kernels: 0 us -> 86 us
  local copies, waits for them, and re-layouts: 46.4 us -> 15.9 us
  starting transfers between devices: 61.9 us -> 34.7 us
  matrix products: 18.8 us -> 0 us
  between operations: 14.8 us -> 0.78 us
  other arithmetic: 20.2 us -> 12.4 us
    ppermute x13 -> x0, waiting for transfers between devices: 272 us -> none  [passed_along(): return lax.ppermute(block, axis, route)]
    unnamed x1 -> x0, blocking collectives: 132 us -> none
    pallas_call x0 -> x1, Pallas kernels: none -> 86 us  [backward(): pl.pallas_call(functools.partial(kernel, nx, ny, nz), out_shape=(jax.Shap...]
    ppermute x13 -> x0, starting transfers between devices: 16.6 us -> none  [passed_along(): return lax.ppermute(block, axis, route)]
    dot_general x6 -> x0, matrix products: 14.4 us -> none  [the longest x2 9.99 us: run_block(): lax.dot_general(normed_block, value_gradient, (((0,), (0,)), ((), ())), p...]
    all_to_all x4, waiting for transfers between devices: 30.4 us -> 43.1 us  [the longest x1 14.5 us: on_device(): lax.all_to_all(out.reshape(TOK, D), 'dp', split_axis=0, concat_axis=0, ti...]
    all_to_all x4, starting transfers between devices: 45.2 us -> 34.7 us  [the longest x1 14.6 us: on_device(): k = regroup(keys)[0]]
    while x26 -> x0, local copies, waits for them, and re-layouts: 9.28 us -> none
  transfers between devices with their start and end apart: 18 -> 4, of which waited for: 17 -> 4; matrix products, arithmetic and copies ran while one was open for 3% -> 10% of each run, Pallas kernels for 0% -> 0%
where the time goes in v1:
time: 194 us; the launch traced here: 193 us
  Pallas kernels  86 us (44%)
  waiting for transfers between devices  43.1 us (22%)
  starting transfers between devices  34.7 us (18%)
  local copies, waits for them, and re-layouts  15.9 us (8%)
  other arithmetic  12.4 us (6%)
    pallas_call x1, Pallas kernels, backward(): pl.pallas_call(functools.partial(kernel, nx, ny, nz), out_shape=(jax.Shap...  86 us
    all_to_all x1, starting transfers between devices, on_device(): k = regroup(keys)[0]  14.6 us
    all_to_all x1, waiting for transfers between devices, on_device(): lax.all_to_all(out.reshape(TOK, D), 'dp', split_axis=0, concat_axis=0, ti...  14.5 us
    all_to_all x1, waiting for transfers between devices, on_device(): q = regroup(queries)[0]  13.3 us
    all_to_all x1, waiting for transfers between devices, on_device(): x = regroup(hidden_in)[0]  11.6 us
    unnamed x19, local copies, waits for them, and re-layouts  11.2 us
    unnamed x4, other arithmetic  9.54 us
    all_to_all x1, starting transfers between devices, on_device(): lax.all_to_all(out.reshape(TOK, D), 'dp', split_axis=0, concat_axis=0, ti...  7.11 us
  transfers between devices with their start and end apart: 4, of which 4 were waited for; matrix products, arithmetic and copies ran while one was open for 10% of the time, Pallas kernels for 0%

profile of v1, /device:TPU:1, one launch (start us, length us, event | category | flops | bytes accessed | tf_op | source)
XLA Modules:
  0.0 192.9 jit_solution(17940919376712814842)
XLA Ops:
  0.6 1.1 copy.31
  1.7 0.5 broadcast.23
  2.3 1.4 reduce.6
  3.7 0.7 reshape.62
  4.4 14.6 %all-to-all-start.2 = ((bf16[64,2,512]{2,1,0:T(2,128)(2,1)}), bf16[64,2,512]{2,1,0:T(2,128)(2,1)S(1)}, u32[]{:S(2)}, u32[]{:S(2)}) async-start(bf16[64,2,512]{2,1,0:T(2,128)(2,1)} %reshape.62), calls=%async_computation.2 | async-start | bytes 262144 | tf_op jit(solution)/shard_map/all_to_all | solution.py:328
  19.0 1.9 copy.30
  20.8 0.0 copy-start
  20.8 3.8 %reduce.5 = bf16[128,2048]{1,0:T(8,128)(2,1)S(1)} reduce(bf16[128,1,2048]{2,1,0:T(2,128)(2,1)S(1)} %bitcast.34, bf16[]{:T(256)} %broadcast.23), dimensions={1}, to_apply=%bitcast.29.reduce_sub_computation | reduce | bytes 1048578
  24.6 1.1 reshape.58
  25.7 3.7 %all-to-all-done.2 = bf16[64,2,512]{2,1,0:T(2,128)(2,1)S(1)} async-done(((bf16[64,2,512]{2,1,0:T(2,128)(2,1)}), bf16[64,2,512]{2,1,0:T(2,128)(2,1)S(1)}, u32[]{:S(2)}, u32[]{:S(2)}) %all-to-all-start.2) | async-done | bytes 131104 | tf_op jit(solution)/shard_map/all_to_all | solution.py:328
  29.4 6.7 %all-to-all-start = ((bf16[64,2,2048]{2,1,0:T(2,128)(2,1)}), bf16[64,2,2048]{2,1,0:T(2,128)(2,1)S(1)}, u32[]{:S(2)}, u32[]{:S(2)}) async-start(bf16[64,2,2048]{2,1,0:T(2,128)(2,1)} %reshape.58), calls=%async_computation | async-start | bytes 1048576 | tf_op jit(solution)/shard_map/all_to_all | solution.py:330
  36.2 0.0 copy-done
  36.2 0.8 copy.29
  37.0 0.0 copy-start.2
  37.0 3.7 %reduce.4 = bf16[128,2048]{1,0:T(8,128)(2,1)S(1)} reduce(bf16[128,1,2048]{2,1,0:T(2,128)(2,1)S(1)} %bitcast.33, bf16[]{:T(256)} %broadcast.23), dimensions={1}, to_apply=%bitcast.28.reduce_sub_computation | reduce | bytes 1048578
  40.7 1.1 reshape.60
  41.9 11.6 %all-to-all-done = bf16[64,2,2048]{2,1,0:T(2,128)(2,1)S(1)} async-done(((bf16[64,2,2048]{2,1,0:T(2,128)(2,1)}), bf16[64,2,2048]{2,1,0:T(2,128)(2,1)S(1)}, u32[]{:S(2)}, u32[]{:S(2)}) %all-to-all-start) | async-done | bytes 524320 | tf_op jit(solution)/shard_map/all_to_all | solution.py:330
  53.5 6.3 %all-to-all-start.1 = ((bf16[64,2,2048]{2,1,0:T(2,128)(2,1)}), bf16[64,2,2048]{2,1,0:T(2,128)(2,1)S(1)}, u32[]{:S(2)}, u32[]{:S(2)}) async-start(bf16[64,2,2048]{2,1,0:T(2,128)(2,1)} %reshape.60), calls=%async_computation.1 | async-start | bytes 1048576 | tf_op jit(solution)/shard_map/all_to_all | solution.py:329
  59.8 0.0 copy-done.2
  59.8 0.7 copy.18.segc_ref
  60.5 0.5 broadcast.22
  61.0 0.7 reduce.3
  61.7 0.1 tile.10
  61.8 0.7 tile.12.segr_ref
  62.5 0.1 reshape.63
  62.6 0.7 copy.28
  63.2 0.5 reshape.59
  63.8 13.3 %all-to-all-done.1 = bf16[64,2,2048]{2,1,0:T(2,128)(2,1)S(1)} async-done(((bf16[64,2,2048]{2,1,0:T(2,128)(2,1)}), bf16[64,2,2048]{2,1,0:T(2,128)(2,1)S(1)}, u32[]{:S(2)}, u32[]{:S(2)}) %all-to-all-start.1) | async-done | bytes 524320 | tf_op jit(solution)/shard_map/all_to_all | solution.py:329
  77.1 0.5 reshape.61
  77.6 1.6 copy_bitcast_fusion
  79.2 86.0 %chain.1 = (bf16[8,16,2048]{2,1,0:T(8,128)(2,1)}, f32[32,512]{1,0:T(8,128)}) custom-call(bf16[128,2048]{1,0:T(8,128)(2,1)} %get-tuple-element.10.x_ref, bf16[128,2048]{1,0:T(8,128)(2,1)} %get-tuple-element.9.q_ref, bf16[128,512]{1,0:T(8,128)(2,1)} %bitcast.39, s32[128,1]{1,0:T(8,128)} %copy.18.segc_ref, s32[2,1,256]{2,1,0:T(1,128)} %tile.12.segr_ref, ...), custom_call_target="tpu_custom_call" | custom-call | tf_op jit(solution)/shard_map/chain/pallas_call | solution.py:289
  165.2 0.0 copy-start.1
  165.2 2.2 %all_to_all.18 = bf16[64,2,2048]{2,1,0:T(2,128)(2,1)} reshape(bf16[8,16,2048]{2,1,0:T(8,128)(2,1)} %get-tuple-element.5) | data formatting | bytes 1048576 | tf_op jit(solution)/shard_map/all_to_all | solution.py:337
  167.4 7.1 %all-to-all-start.3 = ((bf16[64,2,2048]{2,1,0:T(2,128)(2,1)}), bf16[64,2,2048]{2,1,0:T(2,128)(2,1)S(1)}, u32[]{:S(2)}, u32[]{:S(2)}) async-start(bf16[64,2,2048]{2,1,0:T(2,128)(2,1)} %all_to_all.18), calls=%async_computation.3 | async-start | bytes 1048576 | tf_op jit(solution)/shard_map/all_to_all | solution.py:337
  174.6 0.7 multiply_bitcast_fusion.2
  175.3 0.0 copy-done.1
  175.3 1.6 fusion
  176.9 0.5 multiply_bitcast_fusion.1
  177.4 14.5 %all-to-all-done.3 = bf16[64,2,2048]{2,1,0:T(2,128)(2,1)S(1)} async-done(((bf16[64,2,2048]{2,1,0:T(2,128)(2,1)}), bf16[64,2,2048]{2,1,0:T(2,128)(2,1)S(1)}, u32[]{:S(2)}, u32[]{:S(2)}) %all-to-all-start.3) | async-done | bytes 524320 | tf_op jit(solution)/shard_map/all_to_all | solution.py:337
  191.9 1.0 broadcast_in_dim.8
  (1 shorter events, 0.0 us)
Async XLA Ops:
  4.4 25.1 %all-to-all-start.2 = ((bf16[64,2,512]{2,1,0:T(2,128)(2,1)}), bf16[64,2,512]{2,1,0:T(2,128)(2,1)S(1)}, u32[]{:S(2)}, u32[]{:S(2)}) async-start(bf16[64,2,512]{2,1,0:T(2,128)(2,1)} %reshape.62), calls=%async_computation.2 | async-start | bytes 262144 | tf_op jit(solution)/shard_map/all_to_all | solution.py:328
  20.8 15.4 %copy-start = (bf16[1,128,2048]{2,1,0:T(8,128)(2,1)S(1)}, bf16[1,128,2048]{2,1,0:T(8,128)(2,1)}, u32[]{:S(2)}) copy-start(bf16[1,128,2048]{2,1,0:T(8,128)(2,1)} %param.8) | copy-start | bytes 1572868
  29.4 24.1 %all-to-all-start = ((bf16[64,2,2048]{2,1,0:T(2,128)(2,1)}), bf16[64,2,2048]{2,1,0:T(2,128)(2,1)S(1)}, u32[]{:S(2)}, u32[]{:S(2)}) async-start(bf16[64,2,2048]{2,1,0:T(2,128)(2,1)} %reshape.58), calls=%async_computation | async-start | bytes 1048576 | tf_op jit(solution)/shard_map/all_to_all | solution.py:330
  37.0 22.8 %copy-start.2 = (s32[1,128]{1,0:T(1,128)S(1)}, s32[1,128]{1,0:T(1,128)}, u32[]{:S(2)}) copy-start(s32[1,128]{1,0:T(1,128)} %param.10) | copy-start | bytes 1540
  53.5 23.6 %all-to-all-start.1 = ((bf16[64,2,2048]{2,1,0:T(2,128)(2,1)}), bf16[64,2,2048]{2,1,0:T(2,128)(2,1)S(1)}, u32[]{:S(2)}, u32[]{:S(2)}) async-start(bf16[64,2,2048]{2,1,0:T(2,128)(2,1)} %reshape.60), calls=%async_computation.1 | async-start | bytes 1048576 | tf_op jit(solution)/shard_map/all_to_all | solution.py:329
  165.2 10.1 %copy-start.1 = (f32[32,512]{1,0:T(8,128)S(1)}, f32[32,512]{1,0:T(8,128)}, u32[]{:S(2)}) copy-start(f32[32,512]{1,0:T(8,128)} %get-tuple-element.6) | copy-start | bytes 196612
  167.4 24.4 %all-to-all-start.3 = ((bf16[64,2,2048]{2,1,0:T(2,128)(2,1)}), bf16[64,2,2048]{2,1,0:T(2,128)(2,1)S(1)}, u32[]{:S(2)}, u32[]{:S(2)}) async-start(bf16[64,2,2048]{2,1,0:T(2,128)(2,1)} %all_to_all.18), calls=%async_computation.3 | async-start | bytes 1048576 | tf_op jit(solution)/shard_map/all_to_all | solution.py:337

commit v2 on v1

v2 whole, which is shorter than its diff:
```python
import functools

import jax
import jax.numpy as jnp
from jax import lax
from jax.experimental import pallas as pl
from jax.experimental.pallas import tpu as pltpu
from jax.sharding import PartitionSpec as P

HEADS = 16
KV = 4
GROUP = HEADS // KV
HF = 128
D = HEADS * HF
KW = KV * HF
ROWS = 64
MICRO = 2
TOK = ROWS * MICRO
PR = 16
PIECES = TOK // PR
PER = ROWS // PR
EPS = 1e-06
MASKED = -1e30
XS = 4
MESH = pl.DeviceIdType.MESH
F32 = jnp.float32
BF = jnp.bfloat16


def dot(a, b, dims=(((1,), (0,)), ((), ()))):
    return lax.dot_general(a, b, dims, preferred_element_type=F32)


NT = (((1,), (1,)), ((), ()))


def rows_of(i, n):
    return pl.ds(pl.multiple_of(i * n, n), n)


def kernel(
    nx, ny, nz,
    x_in, q_in, k_in, seg_ref, w_ref, gain_ref, up_ref,
    fin_ref, wg_ref, gg_ref,
    ql, kl, xl, out, gin, gs, mask, pt, yv, inv, wt, xs, xst, us, cst, part, gcol, spare,
    up_sem, list_recv, list_send, gin_sem, gout_sem, fin_recv, fin_send,
    xs_recv, xs_send, us_recv, us_send, part_recv, part_send,
):
    me = lax.axis_index("dp")
    sec = lax.axis_index("section")
    core = lax.rem(me, 2)
    my_y = lax.rem(lax.div(me, 2), ny)
    my_x = lax.div(me, 2 * ny)
    last = nz - 1
    ndp = 2 * nx * ny
    pair = TOK // ndp
    slots = 2 * nx
    fw = D // slots
    fo = D // ndp
    slot = my_x * 2 + core
    scale = float(TOK * ndp) ** (-0.5)

    def dev(x, y, c):
        return (x * ny + y) * 2 + c

    def remote(src, dst, send, recv, target, section=None):
        return pltpu.make_async_remote_copy(
            src_ref=src, dst_ref=dst, send_sem=send, recv_sem=recv,
            device_id=(target, sec if section is None else section), device_id_type=MESH,
        )

    barrier = pltpu.get_barrier_semaphore()

    def greet(d, _):
        pl.semaphore_signal(
            barrier, inc=1, device_id=(lax.rem(me + d, ndp), sec), device_id_type=MESH
        )
        return 0

    lax.fori_loop(1, ndp, greet, 0)

    @pl.when(sec > 0)
    def _():
        pl.semaphore_signal(barrier, inc=1, device_id=(me, sec - 1), device_id_type=MESH)

    @pl.when(sec < last)
    def _():
        pl.semaphore_signal(barrier, inc=1, device_id=(me, sec + 1), device_id_type=MESH)

    up_copy = pltpu.make_async_copy(up_ref, gin, up_sem)

    @pl.when(sec == last)
    def _():
        up_copy.start()

    neighbours = (sec > 0).astype(jnp.int32) + (sec < last).astype(jnp.int32)
    pl.semaphore_wait(barrier, ndp - 1 + neighbours)

    arrays = ((k_in, kl), (q_in, ql), (x_in, xl))
    for n, (src, dst) in enumerate(arrays):

        def give(d, _):
            target = lax.rem(me + d, ndp)
            remote(
                src.at[rows_of(target, pair), :], dst.at[rows_of(me, pair), :],
                list_send.at[n], list_recv.at[n], target,
            ).start()
            return 0

        lax.fori_loop(1, ndp, give, 0)
        pltpu.make_async_copy(
            src.at[rows_of(me, pair), :], dst.at[rows_of(me, pair), :], list_recv.at[n]
        ).start()
        pltpu.make_async_copy(
            src.at[rows_of(me, pair), :],
            spare.at[n, pl.ds(0, pair), pl.ds(0, src.shape[1])],
            list_send.at[n],
        ).start()

    def listed(n):
        pltpu.make_async_copy(arrays[n][1], arrays[n][1], list_recv.at[n]).wait()

    gain = gain_ref[...]
    segs = jnp.broadcast_to(seg_ref[...].astype(F32), (GROUP * ROWS, TOK)).astype(BF)

    def lane(shape, axis):
        return lax.broadcasted_iota(jnp.int32, shape, axis)

    for m in range(MICRO):
        pick = (lane((ROWS, TOK), 0) + m * ROWS == lane((ROWS, TOK), 1)).astype(F32).astype(BF)
        key_list = dot(pick, segs, NT)
        wide = (TOK, GROUP * ROWS)
        spread = (lane(wide, 0) == lax.rem(lane(wide, 1), ROWS) + m * ROWS).astype(F32).astype(BF)
        query_list = dot(segs[:ROWS], spread)
        tall = (ROWS, GROUP * ROWS)
        causal = lane(tall, 0) <= lax.rem(lane(tall, 1), ROWS)
        mask[m] = jnp.where((key_list == query_list) & causal, 1.0, 0.0)
    for i in range(D // HF):
        wt[:, i * HF:(i + 1) * HF] = w_ref[i * HF:(i + 1) * HF, :].T
    own = lane((fo, D), 1) == me * fo + lane((fo, D), 0)
    gcol[...] = jnp.sum(jnp.where(own, gain, 0.0), axis=1, keepdims=True)
    gs[...] = jnp.zeros_like(gs)

    listed(0)
    listed(1)

    def probs(m, _):
        allowed = mask[m] > 0.5
        for c in range(KV):
            kc = kl[rows_of(m, ROWS), c * HF:(c + 1) * HF]
            qc = jnp.concatenate(
                [
                    ql[rows_of(m, ROWS), (c * GROUP + h) * HF:(c * GROUP + h + 1) * HF]
                    for h in range(GROUP)
                ],
                axis=0,
            )
            s = dot(kc, qc, NT) * HF ** (-0.5)
            s = jnp.where(allowed, s, MASKED)
            e = jnp.exp(s - jnp.max(s, axis=0, keepdims=True))
            pt[m, c] = (e / jnp.sum(e, axis=0, keepdims=True)).astype(BF)
        return 0

    lax.fori_loop(0, MICRO, probs, 0)

    listed(2)

    def peer(step):
        p = lax.rem(slot + step, slots)
        return p, dev(lax.div(p, 2), my_y, lax.rem(p, 2))

    def columns(p):
        return xl.at[:, pl.ds(pl.multiple_of(p * fw, fw), fw)]

    def x_copy(step):
        p, target = peer(step)
        return remote(columns(p), xs.at[slot], xs_send.at[step], xs_recv, target)

    for step in range(1, slots):
        x_copy(step).start()
    pltpu.make_async_copy(columns(slot), xs.at[slot], xs_recv).start()

    def stats(i, _):
        xf = xl[rows_of(i, PR), :].astype(F32)
        inv[rows_of(i, PR), :] = lax.rsqrt(
            jnp.sum(xf * xf, axis=1, keepdims=True) * (1.0 / D) + EPS
        )
        return 0

    lax.fori_loop(0, PIECES, stats, 0)
    xg = (xl[...].astype(F32) * gain).astype(BF)
    yv[...] = dot(xg, w_ref[...]) * (1.0 / D)

    def turn_x():
        pltpu.make_async_copy(xs, xs, xs_recv).wait()
        for i in range(slots):
            xst[:, i * TOK:(i + 1) * TOK] = xs[i].T

    @pl.when(sec < last)
    def _():
        turn_x()

    @pl.when(sec == last)
    def _():
        up_copy.wait()

    def g_copy(ci):
        return remote(
            out.at[rows_of(ci, PR), :], gin.at[rows_of(ci, PR), :],
            gout_sem.at[ci], gin_sem.at[ci], me, lax.max(sec - 1, 0),
        )

    def u_copy(ci, step):
        _, target = peer(step)
        rows = us.at[slot, rows_of(ci, PR), :]
        return remote(rows, rows, us_send.at[ci, step], us_recv, target)

    def chain(t, _):
        m = lax.rem(t, MICRO)
        b = PER - 1 - lax.div(t, MICRO)
        ci = m * PER + b

        @pl.when(sec < last)
        def _():
            g_copy(ci).wait_recv()

        g = gin[rows_of(ci, PR), :]
        for h in range(HEADS):
            c, hh = divmod(h, GROUP)
            gs[m, c, pl.ds(pl.multiple_of(hh * ROWS + b * PR, PR), PR), :] = g[:, h * HF:(h + 1) * HF]
        v = jnp.concatenate(
            [dot(pt[m, c, rows_of(b, PR), :], gs[m, c]) for c in range(KV)], axis=1
        ).astype(BF)
        r = inv[rows_of(ci, PR), :]
        uf = v.astype(F32) * r
        u = uf.astype(BF)
        coef = jnp.sum(uf * yv[rows_of(ci, PR), :], axis=1, keepdims=True) * (r * r)
        ng = dot(u, wt[...])
        xf = xl[rows_of(ci, PR), :].astype(F32)
        out[rows_of(ci, PR), :] = (g.astype(F32) + (gain * ng - xf * coef)).astype(BF)
        us[slot, rows_of(ci, PR), :] = u

        @pl.when(sec > 0)
        def _():
            g_copy(ci).start()

        for step in range(1, slots):
            u_copy(ci, step).start()

        def back(i, _):
            target = ci * (PR // pair) + i
            src = out.at[rows_of(target, pair), :]
            dst = fin_ref.at[rows_of(me, pair), :]

            @pl.when(target != me)
            def _():
                remote(src, dst, fin_send, fin_recv, target).start()

            @pl.when(target == me)
            def _():
                pltpu.make_async_copy(src, dst, fin_recv).start()
                pltpu.make_async_copy(src, spare.at[3, pl.ds(0, pair), :], fin_send).start()

            return 0

        lax.fori_loop(0, PR // pair, back, 0)
        return 0

    lax.fori_loop(0, PIECES, chain, 0)

    @pl.when(sec == last)
    def _():
        turn_x()

    others = us.at[pl.ds(0, slots - 1)]
    pltpu.make_async_copy(others, others, us_recv).wait()
    acc = dot(xst[...], us[...].reshape(slots * TOK, KW))
    cst[...] = acc.astype(BF).reshape(ny, fo, KW)

    def part_copy(j):
        yl, c = divmod(j, 2)
        target = dev(my_x, core * (ny // 2) + yl, c)
        return target, remote(cst.at[j], part.at[my_y], part_send.at[j], part_recv, target)

    for j in range(ny):
        target, copy = part_copy(j)

        @pl.when(target != me)
        def _():
            copy.start()

        @pl.when(target == me)
        def _():
            pltpu.make_async_copy(cst.at[j], part.at[my_y], part_recv).start()

    pltpu.make_async_copy(part, part, part_recv).wait()
    total = part[0].astype(F32)
    for y in range(1, ny):
        total = total + part[y].astype(F32)
    total = total * scale
    wg_ref[...] = total * gcol[...]
    terms = total * w_ref[rows_of(me, fo), :].astype(F32)
    gg_ref[...] = jnp.sum(terms.T, axis=0, keepdims=True)

    pltpu.make_async_copy(fin_ref, fin_ref, fin_recv).wait()

    pltpu.make_async_copy(out, out, fin_send).wait()
    for n, (_, dst) in enumerate(arrays):
        pltpu.make_async_copy(dst, dst, list_send.at[n]).wait()
    for step in range(1, slots):
        x_copy(step).wait_send()

    def drain(ci, _):
        for step in range(1, slots):
            u_copy(ci, step).wait_send()

        @pl.when(sec > 0)
        def _():
            g_copy(ci).wait_send()

        return 0

    lax.fori_loop(0, PIECES, drain, 0)
    for j in range(ny):
        target, copy = part_copy(j)

        @pl.when(target != me)
        def _():
            copy.wait_send()


def on_device(nx, ny, nz, hidden_in, queries, keys, segments, value_weight, norm_gain, upstream):
    slots = 2 * nx
    ndp = slots * ny
    fw = D // slots
    fo = D // ndp
    pair = TOK // ndp
    vmem = pl.BlockSpec(memory_space=pltpu.VMEM)
    hbm = pl.BlockSpec(memory_space=pl.ANY)
    sem = pltpu.SemaphoreType.DMA
    fin, wg, gg = pl.pallas_call(
        functools.partial(kernel, nx, ny, nz),
        out_shape=(
            jax.ShapeDtypeStruct((TOK, D), BF),
            jax.ShapeDtypeStruct((fo, KW), F32),
            jax.ShapeDtypeStruct((1, fo), F32),
        ),
        in_specs=[hbm] * 3 + [vmem] * 3 + [hbm],
        out_specs=(vmem, vmem, vmem),
        scratch_shapes=[
            pltpu.VMEM((TOK, D), BF),
            pltpu.VMEM((TOK, KW), BF),
            pltpu.VMEM((TOK, D), BF),
            pltpu.VMEM((TOK, D), BF),
            pltpu.VMEM((TOK, D), BF),
            pltpu.VMEM((MICRO, KV, GROUP * ROWS, HF), BF),
            pltpu.VMEM((MICRO, ROWS, GROUP * ROWS), F32),
            pltpu.VMEM((MICRO, KV, ROWS, GROUP * ROWS), BF),
            pltpu.VMEM((TOK, KW), F32),
            pltpu.VMEM((TOK, 1), F32),
            pltpu.VMEM((KW, D), BF),
            pltpu.VMEM((slots, TOK, fw), BF),
            pltpu.VMEM((fw, slots * TOK), BF),
            pltpu.VMEM((slots, TOK, KW), BF),
            pltpu.VMEM((ny, fo, KW), BF),
            pltpu.VMEM((ny, fo, KW), BF),
            pltpu.VMEM((fo, 1), F32),
            pltpu.VMEM((4, max(pair, 16), D), BF),
            sem,
            sem((3,)),
            sem((3,)),
            sem((PIECES,)),
            sem((PIECES,)),
            sem,
            sem,
            sem,
            sem((slots,)),
            sem,
            sem((PIECES, slots)),
            sem,
            sem((ny,)),
        ],
        compiler_params=pltpu.CompilerParams(
            collective_id=0, has_side_effects=True, vmem_limit_bytes=60000 * 1024
        ),
        name="chain",
    )(
        hidden_in[0], queries[0], keys[0], segments, value_weight[0], norm_gain, upstream
    )
    return fin[None], wg[None], gg


def solution(mesh):
    ndp = mesh.shape["dp"]
    nx = XS
    ny = ndp // (2 * nx)
    in_specs = (
        P("section", "dp", None),
        P("section", "dp", None),
        P("section", "dp", None),
        P("dp", None),
        P("section", None, None),
        P("section", None),
        P("dp", None),
    )
    out_specs = (P("section", "dp", None), P("section", "dp", None), P("section", "dp"))
    return jax.shard_map(
        functools.partial(on_device, nx, ny, mesh.shape["section"]),
        mesh=mesh, in_specs=in_specs, out_specs=out_specs, check_vma=False,
    )
```

time: 194 us -> 134 us (0.69)
  waiting for transfers between devices: 43.1 us -> 0 us
  Pallas kernels: 86 us -> 128 us
  starting transfers between devices: 34.7 us -> 0 us
  other arithmetic: 12.4 us -> 0 us
  local copies, waits for them, and re-layouts: 15.9 us -> 4.53 us
    all_to_all x4 -> x0, waiting for transfers between devices: 43.1 us -> none  [the longest x1 14.5 us: on_device(): lax.all_to_all(out.reshape(TOK, D), 'dp', split_axis=0, concat_axis=0, ti...]
    pallas_call x1, Pallas kernels: 86 us -> 128 us  [on_device(): pl.pallas_call(functools.partial(kernel, nx, ny, nz), out_shape=(jax.Shap...]
    all_to_all x4 -> x0, starting transfers between devices: 34.7 us -> none  [the longest x1 14.6 us: on_device(): k = regroup(keys)[0]]
    unnamed x4 -> x0, other arithmetic: 9.54 us -> none
    unnamed x19 -> x3, local copies, waits for them, and re-layouts: 11.2 us -> 4.53 us
    all_to_all x1 -> x0, local copies, waits for them, and re-layouts: 2.2 us -> none  [on_device(): lax.all_to_all(out.reshape(TOK, D), 'dp', split_axis=0, concat_axis=0, ti...]
  transfers between devices with their start and end apart: 4 -> 0, of which waited for: 4 -> 0; matrix products, arithmetic and copies ran while one was open for 10% -> 0% of each run, Pallas kernels for 0% -> 0%
where the time goes in v2:
time: 134 us; the launch traced here: 133 us
  Pallas kernels  128 us (96%)
  local copies, waits for them, and re-layouts  4.53 us (3%)
    pallas_call x1, Pallas kernels, on_device(): pl.pallas_call(functools.partial(kernel, nx, ny, nz), out_shape=(jax.Shap...  128 us
    unnamed x3, local copies, waits for them, and re-layouts  4.53 us

profile of v2, /device:TPU:1, one launch (start us, length us, event | category | flops | bytes accessed | tf_op | source)
XLA Modules:
  0.0 133.1 jit_solution(14490307498631150634)
XLA Ops:
  0.6 127.9 %chain.1 = (bf16[128,2048]{1,0:T(8,128)(2,1)}, f32[32,512]{1,0:T(8,128)}, f32[1,32]{1,0:T(1,128)}) custom-call(bf16[128,2048]{1,0:T(8,128)(2,1)} %bitcast.8, bf16[128,2048]{1,0:T(8,128)(2,1)} %bitcast.9, bf16[128,512]{1,0:T(8,128)(2,1)} %bitcast.10, s32[1,128]{1,0:T(1,128)} %seg_ref.1, bf16[2048,512]{1,0:T(8,128)(2,1)} %bitcast.6, f32[1,2048]{1,0:T(1,128)} %gain_ref.1, ...), custom_call_target="tpu_custom_call" | custom-call | tf_op jit(solution)/shard_map/chain/pallas_call | solution.py:341
  128.6 1.9 %copy.13 = bf16[1,128,2048]{2,1,0:T(8,128)(2,1)} copy(bf16[1,128,2048]{2,1,0:T(8,128)(2,1)} %bitcast.7) | data formatting | bytes 1048576
  130.4 1.5 %copy.14 = f32[1,32,512]{2,1,0:T(8,128)} copy(f32[1,32,512]{2,1,0:T(8,128)} %bitcast.11) | data formatting | bytes 131072
  131.9 1.2 copy.15

commit v3 on v2

--- a/solution.py
+++ b/solution.py
@@ -16,7 +16,7 @@
 ROWS = 64
 MICRO = 2
 TOK = ROWS * MICRO
-PR = 16
+PR = 8
 PIECES = TOK // PR
 PER = ROWS // PR
 EPS = 1e-06
@@ -196,7 +196,7 @@
         for i in range(slots):
             xst[:, i * TOK:(i + 1) * TOK] = xs[i].T
 
-    @pl.when(sec < last)
+    @pl.when(sec < nz // 2)
     def _():
         turn_x()
 
@@ -268,7 +268,7 @@
 
     lax.fori_loop(0, PIECES, chain, 0)
 
-    @pl.when(sec == last)
+    @pl.when(sec >= nz // 2)
     def _():
         turn_x()
 
@@ -327,6 +327,12 @@
         @pl.when(target != me)
         def _():
             copy.wait_send()
+
+
+def finish(fin_ref, wg_ref, gg_ref, input_ref, weight_ref, gain_ref):
+    input_ref[0] = fin_ref[...]
+    weight_ref[0] = wg_ref[...]
+    gain_ref[...] = gg_ref[...]
 
 
 def on_device(nx, ny, nz, hidden_in, queries, keys, segments, value_weight, norm_gain, upstream):
@@ -387,7 +393,17 @@
     )(
         hidden_in[0], queries[0], keys[0], segments, value_weight[0], norm_gain, upstream
     )
-    return fin[None], wg[None], gg
+    return pl.pallas_call(
+        finish,
+        out_shape=(
+            jax.ShapeDtypeStruct((1, TOK, D), BF),
+            jax.ShapeDtypeStruct((1, fo, KW), F32),
+            jax.ShapeDtypeStruct((1, fo), F32),
+        ),
+        in_specs=[vmem] * 3,
+        out_specs=(vmem, vmem, vmem),
+        name="finish",
+    )(fin, wg, gg)
 
 
 def solution(mesh):

time: 134 us -> 124 us (0.925)
  Pallas kernels: 128 us -> 123 us
  local copies, waits for them, and re-layouts: 4.53 us -> 0 us
    pallas_call x1, Pallas kernels: 128 us -> 121 us  [on_device(): pl.pallas_call(functools.partial(kernel, nx, ny, nz), out_shape=(jax.Shap...]
    unnamed x3 -> x0, local copies, waits for them, and re-layouts: 4.53 us -> none
    pallas_call x0 -> x1, Pallas kernels: none -> 1.92 us  [on_device(): pl.pallas_call(finish, out_shape=(jax.ShapeDtypeStruct((1, TOK, D), BF),...]
where the time goes in v3:
time: 124 us
  Pallas kernels  123 us (99%)
    pallas_call x1, Pallas kernels, on_device(): pl.pallas_call(functools.partial(kernel, nx, ny, nz), out_shape=(jax.Shap...  121 us

profile of v3, /device:TPU:1, one launch (start us, length us, event | category | flops | bytes accessed | tf_op | source)
XLA Modules:
  0.0 123.7 jit_solution(7638968139027200509)
XLA Ops:
  0.6 121.2 %chain.1 = (bf16[128,2048]{1,0:T(8,128)(2,1)}, f32[32,512]{1,0:T(8,128)}, f32[1,32]{1,0:T(1,128)}) custom-call(bf16[128,2048]{1,0:T(8,128)(2,1)} %bitcast.5, bf16[128,2048]{1,0:T(8,128)(2,1)} %bitcast.6, bf16[128,512]{1,0:T(8,128)(2,1)} %bitcast.7, s32[1,128]{1,0:T(1,128)} %seg_ref.1, bf16[2048,512]{1,0:T(8,128)(2,1)} %bitcast.4, f32[1,2048]{1,0:T(1,128)} %gain_ref.1, ...), custom_call_target="tpu_custom_call" | custom-call | tf_op jit(solution)/shard_map/chain/pallas_call | solution.py:347
  121.8 1.9 %finish.1 = (bf16[1,128,2048]{2,1,0:T(8,128)(2,1)}, f32[1,32,512]{2,1,0:T(8,128)}, f32[1,32]{1,0:T(1,128)}) custom-call(bf16[128,2048]{1,0:T(8,128)(2,1)} %get-tuple-element.6.fin_ref, f32[32,512]{1,0:T(8,128)} %get-tuple-element.7.wg_ref, f32[1,32]{1,0:T(1,128)} %get-tuple-element.8.gg_ref), custom_call_target="tpu_custom_call" | custom-call | tf_op jit(solution)/shard_map/finish/pallas_call | solution.py:396

commit v4 on v3

--- a/solution.py
+++ b/solution.py
@@ -40,10 +40,10 @@
 
 def kernel(
     nx, ny, nz,
-    x_in, q_in, k_in, seg_ref, w_ref, gain_ref, up_ref,
+    x_in, q_in, k_in, seg_ref, w_in, gain_ref, up_ref,
     fin_ref, wg_ref, gg_ref,
-    ql, kl, xl, out, gin, gs, mask, pt, yv, inv, wt, xs, xst, us, cst, part, gcol, spare,
-    up_sem, list_recv, list_send, gin_sem, gout_sem, fin_recv, fin_send,
+    ql, kl, xl, out, gin, gs, mask, pt, yv, inv, wt, xs, xst, us, cst, part, gcol, spare, w_ref,
+    up_sem, w_sem, list_recv, list_send, gin_sem, gout_sem, fin_recv, fin_send,
     xs_recv, xs_send, us_recv, us_send, part_recv, part_send,
 ):
     me = lax.axis_index("dp")
@@ -87,6 +87,8 @@
     def _():
         pl.semaphore_signal(barrier, inc=1, device_id=(me, sec + 1), device_id_type=MESH)
 
+    w_copy = pltpu.make_async_copy(w_in, w_ref, w_sem)
+    w_copy.start()
     up_copy = pltpu.make_async_copy(up_ref, gin, up_sem)
 
     @pl.when(sec == last)
@@ -135,6 +137,7 @@
         tall = (ROWS, GROUP * ROWS)
         causal = lane(tall, 0) <= lax.rem(lane(tall, 1), ROWS)
         mask[m] = jnp.where((key_list == query_list) & causal, 1.0, 0.0)
+    w_copy.wait()
     for i in range(D // HF):
         wt[:, i * HF:(i + 1) * HF] = w_ref[i * HF:(i + 1) * HF, :].T
     own = lane((fo, D), 1) == me * fo + lane((fo, D), 0)
@@ -180,15 +183,9 @@
         x_copy(step).start()
     pltpu.make_async_copy(columns(slot), xs.at[slot], xs_recv).start()
 
-    def stats(i, _):
-        xf = xl[rows_of(i, PR), :].astype(F32)
-        inv[rows_of(i, PR), :] = lax.rsqrt(
-            jnp.sum(xf * xf, axis=1, keepdims=True) * (1.0 / D) + EPS
-        )
-        return 0
-
-    lax.fori_loop(0, PIECES, stats, 0)
-    xg = (xl[...].astype(F32) * gain).astype(BF)
+    xf = xl[...].astype(F32)
+    inv[...] = lax.rsqrt(jnp.sum(xf * xf, axis=1, keepdims=True) * (1.0 / D) + EPS)
+    xg = (xf * gain).astype(BF)
     yv[...] = dot(xg, w_ref[...]) * (1.0 / D)
 
     def turn_x():
@@ -351,7 +348,7 @@
             jax.ShapeDtypeStruct((fo, KW), F32),
             jax.ShapeDtypeStruct((1, fo), F32),
         ),
-        in_specs=[hbm] * 3 + [vmem] * 3 + [hbm],
+        in_specs=[hbm] * 3 + [vmem, hbm, vmem, hbm],
         out_specs=(vmem, vmem, vmem),
         scratch_shapes=[
             pltpu.VMEM((TOK, D), BF),
@@ -372,6 +369,8 @@
             pltpu.VMEM((ny, fo, KW), BF),
             pltpu.VMEM((fo, 1), F32),
             pltpu.VMEM((4, max(pair, 16), D), BF),
+            pltpu.VMEM((D, KW), BF),
+            sem,
             sem,
             sem((3,)),
             sem((3,)),

time: 124 us -> 122 us (0.984)
  Pallas kernels: 123 us -> 121 us
    pallas_call x1, Pallas kernels: 121 us -> 119 us  [on_device(): pl.pallas_call(functools.partial(kernel, nx, ny, nz), out_shape=(jax.Shap...]
where the time goes in v4:
time: 122 us; the launch traced here: 121 us
  Pallas kernels  121 us (99%)
    pallas_call x1, Pallas kernels, on_device(): pl.pallas_call(functools.partial(kernel, nx, ny, nz), out_shape=(jax.Shap...  119 us

profile of v4, /device:TPU:1, one launch (start us, length us, event | category | flops | bytes accessed | tf_op | source)
XLA Modules:
  0.0 121.4 jit_solution(2428508471616745881)
XLA Ops:
  0.6 118.9 %chain.1 = (bf16[128,2048]{1,0:T(8,128)(2,1)}, f32[32,512]{1,0:T(8,128)}, f32[1,32]{1,0:T(1,128)}) custom-call(bf16[128,2048]{1,0:T(8,128)(2,1)} %bitcast.5, bf16[128,2048]{1,0:T(8,128)(2,1)} %bitcast.6, bf16[128,512]{1,0:T(8,128)(2,1)} %bitcast.7, s32[1,128]{1,0:T(1,128)} %seg_ref.1, bf16[2048,512]{1,0:T(8,128)(2,1)} %bitcast.4, f32[1,2048]{1,0:T(1,128)} %gain_ref.1, ...), custom_call_target="tpu_custom_call" | custom-call | tf_op jit(solution)/shard_map/chain/pallas_call | solution.py:344
  119.5 1.9 %finish.1 = (bf16[1,128,2048]{2,1,0:T(8,128)(2,1)}, f32[1,32,512]{2,1,0:T(8,128)}, f32[1,32]{1,0:T(1,128)}) custom-call(bf16[128,2048]{1,0:T(8,128)(2,1)} %get-tuple-element.6.fin_ref, f32[32,512]{1,0:T(8,128)} %get-tuple-element.7.wg_ref, f32[1,32]{1,0:T(1,128)} %get-tuple-element.8.gg_ref), custom_call_target="tpu_custom_call" | custom-call | tf_op jit(solution)/shard_map/finish/pallas_call | solution.py:395
